TPU v7x, 32 devices: a whole 2x2x4 slice. The times are simulated.
32 devices in a mesh: dp: 8 (over z, y), mp: 4 (over x, core).
Axes of the slice: x: 2, y: 2, z: 4, core: 2. Of those that a mesh axis runs over, the one named last changes fastest.
Arguments:
- activations: bfloat16 [4, 4096, 5120], P(None, 'dp'), may hold values from -60 to 60
- task_weights: bfloat16 [4, 5120, 512], P(None, 'dp', 'mp'), may hold values from -6 to 6
Outputs:
- merged: float32 [5120, 512], P('dp', 'mp')
All inputs are finite; a program needn't handle non-finite values.
Results may differ from a plain program's by a relative error of at most 0.0015.
Values may be sent and summed in bfloat16 or wider, within the bound.
A program may use at most 128 MiB of HBM per device.

v0:
```python
import jax
import jax.numpy as jnp
from jax import lax
from jax.sharding import PartitionSpec as P

ALPHA = 0.9


def dot(left, right, dims):
    return lax.dot_general(left, right, (dims, ((), ())), preferred_element_type=jnp.float32)


def rounded(array):
    return lax.reduce_precision(array, 8, 7)


def split_pair(array):
    coarse = rounded(array)
    high = coarse.astype(jnp.bfloat16)
    low = (array - coarse).astype(jnp.bfloat16)
    return jnp.concatenate([high, low], axis=1)


def shards(activations, task_weights):
    tasks, tokens, width = activations.shape
    cols = task_weights.shape[2]
    total = tasks * tokens * lax.axis_size("dp")
    bf16, f32 = (jnp.bfloat16, jnp.float32)
    flat = activations.reshape(tasks * tokens, width)
    weights = lax.all_gather(task_weights, "dp", axis=1, tiled=True)
    squares = jnp.sum(jnp.square(activations.astype(f32)), axis=1)
    squares_all = jnp.sum(squares, axis=0)[:, None]
    mean = jnp.mean(weights.astype(f32), axis=0)
    mean_pair = split_pair(mean)
    gaps = []
    for task in range(tasks):
        wide = dot(
            activations[task], jnp.concatenate([weights[task], mean_pair], axis=1), ((1,), (0,))
        )
        outputs = rounded(wide[:, :cols])
        gaps.append(outputs - (wide[:, cols : 2 * cols] + wide[:, 2 * cols :]))
    gap = split_pair(jnp.concatenate(gaps, axis=0))
    diag = sum((squares[t][:, None] * (weights[t].astype(f32) - mean) for t in range(tasks)))
    inner = dot(flat, gap, ((0,), (0,)))
    inner = inner[:, :cols] + inner[:, cols:]
    residual = lax.psum_scatter(
        (ALPHA * inner + (1.0 - ALPHA) * diag) / total, "dp", scatter_dimension=0, tiled=True
    )
    full_bf = lax.all_gather(residual.astype(bf16), "dp", axis=0, tiled=True)
    full = full_bf.astype(f32)
    projected = split_pair(dot(flat, full_bf, ((1,), (0,))))
    inner = dot(flat, projected, ((0,), (0,)))
    inner = inner[:, :cols] + inner[:, cols:]
    image = lax.psum_scatter(
        (ALPHA * inner + (1.0 - ALPHA) * squares_all * full) / total,
        "dp",
        scatter_dimension=0,
        tiled=True,
    )
    image_full = lax.all_gather(image.astype(bf16), "dp", axis=0, tiled=True).astype(f32)
    norm0 = jnp.sum(full * full, axis=0)
    alpha0 = norm0 / jnp.sum(full * image_full, axis=0)
    next_full = full - alpha0 * image_full
    norm1 = jnp.sum(next_full * next_full, axis=0)
    beta = norm1 / norm0
    direction = next_full + beta * full
    direction_bf = direction.astype(bf16)
    direction = direction_bf.astype(f32)
    projected = dot(flat, direction_bf, ((1,), (0,)))
    energy = lax.psum(
        (
            ALPHA * jnp.sum(projected * projected, axis=0)
            + (1.0 - ALPHA) * jnp.sum(squares_all * direction * direction, axis=0)
        )
        / total,
        "dp",
    )
    alpha1 = norm1 / energy
    own_mean = jnp.mean(task_weights.astype(f32), axis=0)
    return own_mean + alpha0 * residual + alpha1 * (residual - alpha0 * image + beta * residual)


def solution(mesh):
    return jax.shard_map(
        shards,
        mesh=mesh,
        in_specs=(P(None, "dp", None), P(None, "dp", "mp")),
        out_specs=P("dp", "mp"),
        check_vma=False,
    )
```

profile of v0, /device:TPU:0, one launch (start us, length us, event | category | flops | bytes accessed | tf_op | source)
XLA Modules:
  0.0 432.0 jit_solution(4052554290245626200)
XLA Ops:
  6.5 2.2 copy.6
  8.8 9.5 %fusion = (f32[5120]{0:T(1024)S(1)}, f32[4,5120]{1,0:T(4,128)S(1)}) fusion(bf16[4,512,5120]{2,1,0:T(8,128)(2,1)} %param.2), kind=kLoop, calls=%fused_computation.1 | loop fusion | flops 41917440 | bytes 21073920 | tf_op jit(solution)/shard_map/reduce_sum | solution.py:32
  18.3 0.7 fusion.62
  18.9 79.0 %all-gather.4.cloned.1.call-done = bf16[4,5120,128]{1,2,0:T(8,128)(2,1)} async-done(((bf16[4,640,128]{1,2,0:T(8,128)(2,1)}), bf16[4,5120,128]{1,2,0:T(8,128)(2,1)}) %all-gather.4.cloned.1.call-update) | async-done | bytes 5242896 | tf_op jit(solution)/shard_map/all_gather | solution.py:30
  97.9 3.8 convert_reduce_fusion
  101.8 0.5 reduce-precision_convert_fusion
  102.3 2.1 slice_bitcast_fusion.3
  104.4 6.9 %fusion.30 = f32[512,384]{0,1:T(8,128)} fusion(bf16[4,512,5120]{2,1,0:T(8,128)(2,1)} %param.2, bf16[5120,128]{0,1:T(8,128)(2,1)S(1)} %get-tuple-element.16, bf16[5120,128]{0,1:T(8,128)(2,1)S(1)} %get-tuple-element.15, bf16[5120,128]{0,1:T(8,128)(2,1)} %get-tuple-element.11), kind=kOutput, calls=%fused_computation.65 | convolution fusion | flops 2025062400 | bytes 9961472 | tf_op jit(solution)/shard_map/dot_general | solution.py:10
  111.3 1.3 slice-done.4
  112.6 4.7 %fusion.33 = f32[512,384]{0,1:T(8,128)} fusion(bf16[4,512,5120]{2,1,0:T(8,128)(2,1)S(1)} %bitcast.65, bf16[5120,128]{0,1:T(8,128)(2,1)S(1)} %get-tuple-element.16, bf16[5120,128]{0,1:T(8,128)(2,1)S(1)} %get-tuple-element.15, bf16[5120,128]{0,1:T(8,128)(2,1)} %get-tuple-element.14), kind=kOutput, calls=%fused_computation.66 | convolution fusion | flops 2025062400 | bytes 9961472 | tf_op jit(solution)/shard_map/dot_general | solution.py:10
  117.2 3.7 fusion.36
  120.9 3.3 fusion.39
  124.2 1.6 fusion.53
  126.0 0.2 reduce-precision_convert_fusion.2
  126.2 7.6 %convolution_bitcast_fusion.1 = f32[5120,256]{0,1:T(8,128)} fusion(bf16[2048,5120]{1,0:T(8,128)(2,1)S(1)} %bitcast.66, bf16[2048,128]{0,1:T(8,128)(2,1)S(1)} %get-tuple-element.20, bf16[2048,128]{0,1:T(8,128)(2,1)S(1)} %get-tuple-element.19), kind=kOutput, calls=%fused_computation.5 | convolution fusion | flops 5370806272 | bytes 27262976 | tf_op jit(solution)/shard_map/dot_general | solution.py:10
  133.8 6.0 %fusion.29 = f32[5120,128]{0,1:T(8,128)} fusion(f32[5120,256]{0,1:T(8,128)} %convolution_bitcast_fusion.1, f32[5120,128]{0,1:T(8,128)S(1)} %convert_reduce_fusion, f32[5120]{0:T(1024)S(1)} %bitcast.68, f32[5120]{0:T(1024)S(1)} %bitcast.69, f32[5120]{0:T(1024)S(1)} %bitcast.70, f32[5120]{0:T(1024)S(1)} %bitcast.67, ...), kind=kLoop, calls=%fused_computation.52 | loop fusion | flops 13762560 | bytes 15810560 | tf_op jit(solution)/shard_map/div | solution.py:47
  139.9 69.6 %reduce-scatter.3.cloned.1.call-done = f32[640,128]{0,1:T(8,128)} async-done(((f32[5120,128]{0,1:T(8,128)}), f32[640,128]{0,1:T(8,128)}) %reduce-scatter.3.cloned.1.call-update) | async-done | bytes 327696 | tf_op jit(solution)/shard_map/reduce_scatter | solution.py:46
  209.4 1.7 convert_element_type.68
  211.2 42.2 %all-gather.6.cloned.1.call-done = bf16[5120,128]{0,1:T(8,128)(2,1)} async-done(((bf16[640,128]{0,1:T(8,128)(2,1)}), bf16[5120,128]{0,1:T(8,128)(2,1)}) %all-gather.6.cloned.1.call-update) | async-done | bytes 1310736 | tf_op jit(solution)/shard_map/all_gather | solution.py:49
  253.4 11.6 %reduce-precision_convert_fusion.1 = (bf16[2048,128]{0,1:T(8,128)(2,1)S(1)}, bf16[2048,128]{0,1:T(8,128)(2,1)S(1)}) fusion(bf16[5120,128]{0,1:T(8,128)(2,1)} %all-gather.6.cloned.1.call-done, bf16[2048,5120]{1,0:T(8,128)(2,1)} %bitcast.61), kind=kOutput, calls=%fused_computation.57 | convolution fusion | flops 2685403136 | bytes 23330816 | tf_op jit(solution)/shard_map/dot_general | solution.py:10
  265.0 10.0 %convolution_bitcast_fusion = f32[5120,256]{0,1:T(8,128)S(1)} fusion(bf16[2048,5120]{1,0:T(8,128)(2,1)} %bitcast.62, bf16[2048,128]{0,1:T(8,128)(2,1)S(1)} %get-tuple-element.18, bf16[2048,128]{0,1:T(8,128)(2,1)S(1)} %get-tuple-element.17), kind=kOutput, calls=%fused_computation.4 | convolution fusion | flops 5370806272 | bytes 27262976 | tf_op jit(solution)/shard_map/dot_general | solution.py:10
  275.0 2.0 fusion.22
  277.1 69.6 %reduce-scatter.5.cloned.1.call-done = f32[640,128]{0,1:T(8,128)} async-done(((f32[5120,128]{0,1:T(8,128)}), f32[640,128]{0,1:T(8,128)}) %reduce-scatter.5.cloned.1.call-update) | async-done | bytes 327696 | tf_op jit(solution)/shard_map/reduce_scatter | solution.py:54
  346.6 1.7 convert_element_type.72
  348.6 41.8 %all-gather.8.cloned.1.call-done = bf16[5120,128]{0,1:T(8,128)(2,1)} async-done(((bf16[640,128]{0,1:T(8,128)(2,1)}), bf16[5120,128]{0,1:T(8,128)(2,1)}) %all-gather.8.cloned.1.call-update) | async-done | bytes 1310736 | tf_op jit(solution)/shard_map/all_gather | solution.py:60
  390.4 2.0 fusion.23
  392.5 0.7 multiply_reduce_fusion
  393.1 1.1 fusion.19
  394.3 11.1 %fusion.42 = f32[128]{0:T(128)S(1)} fusion(bf16[5120,128]{0,1:T(8,128)(2,1)S(1)} %get-tuple-element.10, bf16[2048,5120]{1,0:T(8,128)(2,1)} %bitcast.63), kind=kOutput, calls=%fused_computation.69 | convolution fusion | flops 2684878848 | bytes 22282752 | tf_op jit(solution)/shard_map/dot_general | solution.py:10
  405.4 19.0 %psum.7 = f32[128]{0:T(128)S(1)} all-reduce(f32[128]{0:T(128)S(1)} %add_multiply_fusion), channel_id=1, replica_groups=mesh['dp'=8,'mp'=4] {'dp'}, use_global_device_ids=true, to_apply=%region_11.0 | all-reduce | flops 128 | bytes 1024 | tf_op jit(solution)/shard_map/psum | solution.py:70
  424.4 0.2 multiply_add_fusion
  424.6 0.9 copy.7
  (44 shorter events, 0.8 us)
Async XLA Ops:
  6.5 91.4 %all-gather.4.cloned.1.call-start = ((), (), s32[]{:S(2)}) async-start(), calls=%async_computation.2 | async-start | bytes 5898240 | tf_op jit(solution)/shard_map/all_gather | solution.py:30
  8.8 200.7 %reduce-scatter.3.cloned.1.call-start = ((), (), s32[]{:S(2)}) async-start(), calls=%async_computation.3 | async-start | bytes 2949120 | tf_op jit(solution)/shard_map/reduce_scatter | solution.py:46
  97.9 4.3 copy-start
  101.7 9.5 %slice-start = ((s8[20971520]{0:T(1024)(128)(4,1)}), s8[4194304]{0:T(1024)(128)(4,1)S(1)}, s32[]{:S(2)}) async-start(s8[20971520]{0:T(1024)(128)(4,1)} %bitcast.64), calls=%async_computation.7 | async-start | bytes 8388608
  102.2 9.0 %slice-start.1 = ((s8[20971520]{0:T(1024)(128)(4,1)}), s8[4194304]{0:T(1024)(128)(4,1)S(1)}, s32[]{:S(2)}) async-start(s8[20971520]{0:T(1024)(128)(4,1)} %bitcast.64), calls=%async_computation.8 | async-start | bytes 8388608
  102.3 9.0 %slice-start.2 = ((s8[20971520]{0:T(1024)(128)(4,1)}), s8[4194304]{0:T(1024)(128)(4,1)S(1)}, s32[]{:S(2)}) async-start(s8[20971520]{0:T(1024)(128)(4,1)} %bitcast.64), calls=%async_computation.9 | async-start | bytes 8388608
  104.4 6.9 %slice-start.3 = ((s8[20971520]{0:T(1024)(128)(4,1)}), s8[4194304]{0:T(1024)(128)(4,1)S(1)}, s32[]{:S(2)}) async-start(s8[20971520]{0:T(1024)(128)(4,1)} %bitcast.64), calls=%async_computation.10 | async-start | bytes 8388608
  104.4 8.2 %slice-start.4 = ((s8[20971520]{0:T(1024)(128)(4,1)}), s8[4194304]{0:T(1024)(128)(4,1)S(1)}, s32[]{:S(2)}) async-start(s8[20971520]{0:T(1024)(128)(4,1)} %bitcast.64), calls=%async_computation.11 | async-start | bytes 8388608
  124.2 1.6 copy-start.6
  126.1 7.6 %copy-start.7 = (f32[1,5120]{1,0:T(1,128)S(1)}, f32[1,5120]{1,0:T(1,128)}, u32[]{:S(2)}) copy-start(f32[1,5120]{1,0:T(1,128)} %get-tuple-element.24) | copy-start | bytes 61444
  139.8 113.5 %all-gather.6.cloned.1.call-start = ((), (), s32[]{:S(2)}) async-start(), calls=%async_computation.4 | async-start | bytes 1474560 | tf_op jit(solution)/shard_map/all_gather | solution.py:49
  211.1 135.5 %reduce-scatter.5.cloned.1.call-start = ((), (), s32[]{:S(2)}) async-start(), calls=%async_computation.5 | async-start | bytes 2949120 | tf_op jit(solution)/shard_map/reduce_scatter | solution.py:54
  265.0 10.0 %copy-start.1 = (bf16[5120,128]{0,1:T(8,128)(2,1)S(1)}, bf16[5120,128]{0,1:T(8,128)(2,1)}, u32[]{:S(2)}) copy-start(bf16[5120,128]{0,1:T(8,128)(2,1)} %all-gather.6.cloned.1.call-done) | copy-start | bytes 3932164
  277.0 71.3 %copy-start.3 = (bf16[4,640,128]{2,1,0:T(8,128)(2,1)S(1)}, bf16[4,640,128]{2,1,0:T(8,128)(2,1)}, u32[]{:S(2)}) copy-start(bf16[4,640,128]{2,1,0:T(8,128)(2,1)} %param.3) | copy-start | bytes 1966084
  277.0 113.4 %all-gather.8.cloned.1.call-start = ((), (), s32[]{:S(2)}) async-start(), calls=%async_computation.6 | async-start | bytes 1474560 | tf_op jit(solution)/shard_map/all_gather | solution.py:60
  390.4 2.0 copy-start.2
  394.3 30.2 %copy-start.4 = (f32[640,128]{0,1:T(8,128)S(1)}, f32[640,128]{0,1:T(8,128)}, u32[]{:S(2)}) copy-start(f32[640,128]{0,1:T(8,128)} %reduce-scatter.3.cloned.1.call-done) | copy-start | bytes 983044
  394.3 30.1 %copy-start.5 = (f32[640,128]{0,1:T(8,128)S(1)}, f32[640,128]{0,1:T(8,128)}, u32[]{:S(2)}) copy-start(f32[640,128]{0,1:T(8,128)} %reduce-scatter.5.cloned.1.call-done) | copy-start | bytes 983044
Sparse Core Ops, SparseCore 0:
  9.5 88.3 all-gather.3
  139.9 69.4 reduce-scatter.2
  211.7 41.6 all-gather.5
  277.2 69.4 reduce-scatter.4
  348.7 41.6 all-gather.7
where the time goes:
time: 432 us
  waiting for transfers between devices  302 us (70%)
  matrix products  58.9 us (14%)
  other arithmetic  31.1 us (7%)
  blocking collectives  19 us (4%)
  between operations  13.3 us (3%)
  local copies, waits for them, and re-layouts  7.36 us (2%)
    all_gather x1, waiting for transfers between devices, shards(): weights = lax.all_gather(task_weights, 'dp', axis=1, tiled=True)  79 us
    reduce_scatter x1, waiting for transfers between devices, shards(): lax.psum_scatter((ALPHA * inner + (1.0 - ALPHA) * diag) / total, 'dp', sc...  69.6 us
    reduce_scatter x1, waiting for transfers between devices, shards(): lax.psum_scatter((ALPHA * inner + (1.0 - ALPHA) * squares_all * full) / t...  69.6 us
    dot_general x8, matrix products, dot(): lax.dot_general(left, right, (dims, ((), ())), preferred_element_type=jnp...  58.9 us
    all_gather x1, waiting for transfers between devices, shards(): full_bf = lax.all_gather(residual.astype(bf16), 'dp', axis=0, tiled=True)  42.2 us
    all_gather x1, waiting for transfers between devices, shards(): lax.all_gather(image.astype(bf16), 'dp', axis=0, tiled=True).astype(f32)  41.8 us
    psum x1, blocking collectives, shards(): lax.psum((ALPHA * jnp.sum(projected * projected, axis=0) + (1.0 - ALPHA)...  19 us
    reduce_sum x1, other arithmetic, shards(): squares_all = jnp.sum(squares, axis=0)[:, None]  9.47 us
  transfers between devices with their start and end apart: 5, of which 5 were waited for; matrix products, arithmetic and copies ran while one was open for 2% of the time, Pallas kernels for 0%

commit v1 on v0

--- a/solution.py
+++ b/solution.py
@@ -27,7 +27,23 @@
     total = tasks * tokens * lax.axis_size("dp")
     bf16, f32 = (jnp.bfloat16, jnp.float32)
     flat = activations.reshape(tasks * tokens, width)
-    weights = lax.all_gather(task_weights, "dp", axis=1, tiled=True)
+    ways, here, hop = (lax.axis_size("dp"), lax.axis_index("dp"), task_weights.shape[1])
+    shape = [n * ways if d == 1 else n for d, n in enumerate(task_weights.shape)]
+    full_2 = lax.dynamic_update_slice_in_dim(
+        jnp.zeros(shape, task_weights.dtype), task_weights, here * hop, axis=1
+    )
+    going_up = going_down = task_weights
+    for far in range(1, ways // 2 + 1):
+        going_up = lax.ppermute(going_up, "dp", [(d, (d + 1) % ways) for d in range(ways)])
+        full_2 = lax.dynamic_update_slice_in_dim(
+            full_2, going_up, (here - far) % ways * hop, axis=1
+        )
+        if 2 * far < ways:
+            going_down = lax.ppermute(going_down, "dp", [(d, (d - 1) % ways) for d in range(ways)])
+            full_2 = lax.dynamic_update_slice_in_dim(
+                full_2, going_down, (here + far) % ways * hop, axis=1
+            )
+    weights = full_2
     squares = jnp.sum(jnp.square(activations.astype(f32)), axis=1)
     squares_all = jnp.sum(squares, axis=0)[:, None]
     mean = jnp.mean(weights.astype(f32), axis=0)

time: 432 us -> 458 us (1.060)
  starting transfers between devices: 0.17 us -> 16.8 us
  local copies, waits for them, and re-layouts: 7.36 us -> 21.1 us
  waiting for transfers between devices: 302 us -> 295 us
    all_gather x1 -> x0, waiting for transfers between devices: 79 us -> none  [shards(): weights = lax.all_gather(task_weights, 'dp', axis=1, tiled=True)]
    ppermute x0 -> x7, waiting for transfers between devices: none -> 73 us  [the longest x4 48.6 us: shards(): lax.ppermute(going_up, 'dp', [(d, (d + 1) % ways) for d in range(ways)])]
    ppermute x0 -> x7, starting transfers between devices: none -> 16.7 us  [the longest x4 10.5 us: shards(): lax.ppermute(going_up, 'dp', [(d, (d + 1) % ways) for d in range(ways)])]
    dynamic_update_slice x0 -> x8, local copies, waits for them, and re-layouts: none -> 9.85 us  [the longest x3 5.05 us: shards(): lax.dynamic_update_slice_in_dim(full_2, going_down, (here + far) % ways *...]
  transfers between devices with their start and end apart: 5 -> 11, of which waited for: 5 -> 9; matrix products, arithmetic and copies ran while one was open for 2% -> 5% of each run, Pallas kernels for 0% -> 0%
where the time goes in v1:
time: 458 us
  waiting for transfers between devices  295 us (64%)
  matrix products  60.9 us (13%)
  other arithmetic  31.1 us (7%)
  local copies, waits for them, and re-layouts  21.1 us (5%)
  blocking collectives  19 us (4%)
  starting transfers between devices  16.8 us (4%)
  between operations  13.4 us (3%)
    reduce_scatter x1, waiting for transfers between devices, shards(): lax.psum_scatter((ALPHA * inner + (1.0 - ALPHA) * squares_all * full) / t...  69.7 us
    reduce_scatter x1, waiting for transfers between devices, shards(): lax.psum_scatter((ALPHA * inner + (1.0 - ALPHA) * diag) / total, 'dp', sc...  68.5 us
    dot_general x8, matrix products, dot(): lax.dot_general(left, right, (dims, ((), ())), preferred_element_type=jnp...  60.9 us
    ppermute x4, waiting for transfers between devices, shards(): lax.ppermute(going_up, 'dp', [(d, (d + 1) % ways) for d in range(ways)])  48.6 us
    all_gather x1, waiting for transfers between devices, shards(): full_bf = lax.all_gather(residual.astype(bf16), 'dp', axis=0, tiled=True)  42.2 us
    all_gather x1, waiting for transfers between devices, shards(): lax.all_gather(image.astype(bf16), 'dp', axis=0, tiled=True).astype(f32)  41.9 us
    ppermute x3, waiting for transfers between devices, shards(): lax.ppermute(going_down, 'dp', [(d, (d - 1) % ways) for d in range(ways)])  24.5 us
    psum x1, blocking collectives, shards(): lax.psum((ALPHA * jnp.sum(projected * projected, axis=0) + (1.0 - ALPHA)...  19 us
  transfers between devices with their start and end apart: 11, of which 9 were waited for; matrix products, arithmetic and copies ran while one was open for 5% of the time, Pallas kernels for 0%

profile of v1, /device:TPU:0, one launch (start us, length us, event | category | flops | bytes accessed | tf_op | source)
XLA Modules:
  0.0 457.6 jit_solution(15455807735661261472)
XLA Ops:
  7.9 3.0 collective-permute-start
  11.0 3.1 collective-permute-start.1
  14.1 24.9 %collective-permute-done = bf16[4,640,128]{1,2,0:T(8,128)(2,1)S(1)} collective-permute-done((bf16[4,640,128]{1,2,0:T(8,128)(2,1)S(1)}, bf16[4,640,128]{1,2,0:T(8,128)(2,1)S(1)}, u32[]{:S(2)}, u32[]{:S(2)}) %collective-permute-start) | collective-permute-done | bytes 655392 | tf_op jit(solution)/shard_map/ppermute | solution.py:37
  39.0 2.5 collective-permute-start.2
  41.5 9.5 %fusion = (f32[5120]{0:T(1024)S(1)}, f32[4,5120]{1,0:T(4,128)S(1)}) fusion(bf16[4,512,5120]{2,1,0:T(8,128)(2,1)} %param.2), kind=kLoop, calls=%fused_computation.1 | loop fusion | flops 41917440 | bytes 21073920 | tf_op jit(solution)/shard_map/reduce_sum | solution.py:48
  51.0 3.1 collective-permute-start.3
  54.1 14.6 %collective-permute-done.2 = bf16[4,640,128]{1,2,0:T(8,128)(2,1)S(1)} collective-permute-done((bf16[4,640,128]{1,2,0:T(8,128)(2,1)S(1)}, bf16[4,640,128]{1,2,0:T(8,128)(2,1)S(1)}, u32[]{:S(2)}, u32[]{:S(2)}) %collective-permute-start.2) | collective-permute-done | bytes 655392 | tf_op jit(solution)/shard_map/ppermute | solution.py:37
  68.7 2.5 collective-permute-start.4
  71.8 14.8 %collective-permute-done.3 = bf16[4,640,128]{1,2,0:T(8,128)(2,1)} collective-permute-done((bf16[4,640,128]{1,2,0:T(8,128)(2,1)S(1)}, bf16[4,640,128]{1,2,0:T(8,128)(2,1)}, u32[]{:S(2)}, u32[]{:S(2)}) %collective-permute-start.3) | collective-permute-done | bytes 655392 | tf_op jit(solution)/shard_map/ppermute | solution.py:42
  86.6 3.0 broadcast_in_dim.2
  90.5 9.0 %collective-permute-done.4 = bf16[4,640,128]{1,2,0:T(8,128)(2,1)S(1)} collective-permute-done((bf16[4,640,128]{1,2,0:T(8,128)(2,1)S(1)}, bf16[4,640,128]{1,2,0:T(8,128)(2,1)S(1)}, u32[]{:S(2)}, u32[]{:S(2)}) %collective-permute-start.4) | collective-permute-done | bytes 655392 | tf_op jit(solution)/shard_map/ppermute | solution.py:37
  99.6 2.5 collective-permute-start.6
  104.9 2.0 constant_dynamic-update-slice_fusion.3
  107.9 9.7 %collective-permute-done.5 = bf16[4,640,128]{1,2,0:T(8,128)(2,1)} collective-permute-done((bf16[4,640,128]{1,2,0:T(8,128)(2,1)}, bf16[4,640,128]{1,2,0:T(8,128)(2,1)}, u32[]{:S(2)}, u32[]{:S(2)}) %collective-permute-start.5) | collective-permute-done | bytes 655392 | tf_op jit(solution)/shard_map/ppermute | solution.py:42
  117.6 2.0 constant_dynamic-update-slice_fusion.1
  120.6 4.2 slice_bitcast_fusion.3
  124.8 3.8 convert_reduce_fusion
  130.6 7.0 %fusion.30 = f32[512,384]{0,1:T(8,128)} fusion(bf16[4,512,5120]{2,1,0:T(8,128)(2,1)} %param.2, bf16[5120,128]{0,1:T(8,128)(2,1)} %get-tuple-element.16, bf16[5120,128]{0,1:T(8,128)(2,1)} %get-tuple-element.15, bf16[5120,128]{0,1:T(8,128)(2,1)} %get-tuple-element.11), kind=kOutput, calls=%fused_computation.65 | convolution fusion | flops 2025062400 | bytes 9961472 | tf_op jit(solution)/shard_map/dot_general | solution.py:10
  137.6 4.8 %fusion.33 = f32[512,384]{0,1:T(8,128)} fusion(bf16[4,512,5120]{2,1,0:T(8,128)(2,1)S(1)} %bitcast.65, bf16[5120,128]{0,1:T(8,128)(2,1)} %get-tuple-element.16, bf16[5120,128]{0,1:T(8,128)(2,1)} %get-tuple-element.15, bf16[5120,128]{0,1:T(8,128)(2,1)S(1)} %get-tuple-element.14), kind=kOutput, calls=%fused_computation.66 | convolution fusion | flops 2025062400 | bytes 9961472 | tf_op jit(solution)/shard_map/dot_general | solution.py:10
  142.4 4.1 fusion.36
  146.6 4.6 %fusion.39 = f32[512,384]{0,1:T(8,128)} fusion(bf16[4,512,5120]{2,1,0:T(8,128)(2,1)S(1)} %bitcast.65, bf16[5120,128]{0,1:T(8,128)(2,1)} %get-tuple-element.16, bf16[5120,128]{0,1:T(8,128)(2,1)S(1)} %copy-done.3, bf16[5120,128]{0,1:T(8,128)(2,1)S(1)} %get-tuple-element.12), kind=kOutput, calls=%fused_computation.68 | convolution fusion | flops 2025062400 | bytes 9961472 | tf_op jit(solution)/shard_map/dot_general | solution.py:10
  152.7 7.6 %convolution_bitcast_fusion.1 = f32[5120,256]{0,1:T(8,128)} fusion(bf16[2048,5120]{1,0:T(8,128)(2,1)S(1)} %bitcast.66, bf16[2048,128]{0,1:T(8,128)(2,1)S(1)} %get-tuple-element.20, bf16[2048,128]{0,1:T(8,128)(2,1)S(1)} %get-tuple-element.19), kind=kOutput, calls=%fused_computation.5 | convolution fusion | flops 5370806272 | bytes 27262976 | tf_op jit(solution)/shard_map/dot_general | solution.py:10
  160.3 6.0 %fusion.29 = f32[5120,128]{0,1:T(8,128)} fusion(f32[5120,256]{0,1:T(8,128)} %convolution_bitcast_fusion.1, f32[5120,128]{0,1:T(8,128)S(1)} %convert_reduce_fusion, f32[5120]{0:T(1024)S(1)} %bitcast.68, f32[5120]{0:T(1024)S(1)} %bitcast.69, f32[5120]{0:T(1024)S(1)} %bitcast.70, f32[5120]{0:T(1024)S(1)} %bitcast.67, ...), kind=kLoop, calls=%fused_computation.52 | loop fusion | flops 13762560 | bytes 15810560 | tf_op jit(solution)/shard_map/div | solution.py:63
  166.4 68.5 %reduce-scatter.3.cloned.1.call-done = f32[640,128]{0,1:T(8,128)} async-done(((f32[5120,128]{0,1:T(8,128)}), f32[640,128]{0,1:T(8,128)}) %reduce-scatter.3.cloned.1.call-update) | async-done | bytes 327696 | tf_op jit(solution)/shard_map/reduce_scatter | solution.py:62
  236.6 42.2 %all-gather.3.cloned.1.call-done = bf16[5120,128]{0,1:T(8,128)(2,1)} async-done(((bf16[640,128]{0,1:T(8,128)(2,1)}), bf16[5120,128]{0,1:T(8,128)(2,1)}) %all-gather.3.cloned.1.call-update) | async-done | bytes 1310736 | tf_op jit(solution)/shard_map/all_gather | solution.py:65
  278.8 11.6 %reduce-precision_convert_fusion.1 = (bf16[2048,128]{0,1:T(8,128)(2,1)S(1)}, bf16[2048,128]{0,1:T(8,128)(2,1)S(1)}) fusion(bf16[5120,128]{0,1:T(8,128)(2,1)} %all-gather.3.cloned.1.call-done, bf16[2048,5120]{1,0:T(8,128)(2,1)} %bitcast.61), kind=kOutput, calls=%fused_computation.57 | convolution fusion | flops 2685403136 | bytes 23330816 | tf_op jit(solution)/shard_map/dot_general | solution.py:10
  290.4 10.0 %convolution_bitcast_fusion = f32[5120,256]{0,1:T(8,128)S(1)} fusion(bf16[2048,5120]{1,0:T(8,128)(2,1)} %bitcast.62, bf16[2048,128]{0,1:T(8,128)(2,1)S(1)} %get-tuple-element.18, bf16[2048,128]{0,1:T(8,128)(2,1)S(1)} %get-tuple-element.17), kind=kOutput, calls=%fused_computation.4 | convolution fusion | flops 5370806272 | bytes 27262976 | tf_op jit(solution)/shard_map/dot_general | solution.py:10
  300.4 2.0 fusion.22
  302.5 69.7 %reduce-scatter.5.cloned.1.call-done = f32[640,128]{0,1:T(8,128)} async-done(((f32[5120,128]{0,1:T(8,128)}), f32[640,128]{0,1:T(8,128)}) %reduce-scatter.5.cloned.1.call-update) | async-done | bytes 327696 | tf_op jit(solution)/shard_map/reduce_scatter | solution.py:70
  374.1 41.9 %all-gather.5.cloned.1.call-done = bf16[5120,128]{0,1:T(8,128)(2,1)} async-done(((bf16[640,128]{0,1:T(8,128)(2,1)}), bf16[5120,128]{0,1:T(8,128)(2,1)}) %all-gather.5.cloned.1.call-update) | async-done | bytes 1310736 | tf_op jit(solution)/shard_map/all_gather | solution.py:76
  419.8 11.1 %fusion.42 = f32[128]{0:T(128)S(1)} fusion(bf16[5120,128]{0,1:T(8,128)(2,1)S(1)} %get-tuple-element.10, bf16[2048,5120]{1,0:T(8,128)(2,1)} %bitcast.63), kind=kOutput, calls=%fused_computation.69 | convolution fusion | flops 2684878848 | bytes 22282752 | tf_op jit(solution)/shard_map/dot_general | solution.py:10
  431.0 19.0 %psum.7 = f32[128]{0:T(128)S(1)} all-reduce(f32[128]{0:T(128)S(1)} %add_multiply_fusion), channel_id=1, replica_groups=mesh['dp'=8,'mp'=4] {'dp'}, use_global_device_ids=true, to_apply=%region_11.12 | all-reduce | flops 128 | bytes 1024 | tf_op jit(solution)/shard_map/psum | solution.py:86
  (68 shorter events, 20.0 us)
Async XLA Ops:
  6.5 228.3 %reduce-scatter.3.cloned.1.call-start = ((), (), s32[]{:S(2)}) async-start(), calls=%async_computation.2 | async-start | bytes 2949120 | tf_op jit(solution)/shard_map/reduce_scatter | solution.py:62
  7.9 31.1 %collective-permute-start = (bf16[4,640,128]{1,2,0:T(8,128)(2,1)S(1)}, bf16[4,640,128]{1,2,0:T(8,128)(2,1)S(1)}, u32[]{:S(2)}, u32[]{:S(2)}) collective-permute-start(bf16[4,640,128]{1,2,0:T(8,128)(2,1)S(1)} %copy.8), channel_id=1, source_target_pairs={{0,4},{4,8},{8,12},{12,16},{16,20},{20,24},{24,28},{28,0},{1,5},{5... | collective-permute-start | bytes 1966088 | tf_op jit(solution)/shard_map/ppermute | solution.py:37
  11.0 40.0 %collective-permute-start.1 = (bf16[4,640,128]{1,2,0:T(8,128)(2,1)S(1)}, bf16[4,640,128]{1,2,0:T(8,128)(2,1)S(1)}, u32[]{:S(2)}, u32[]{:S(2)}) collective-permute-start(bf16[4,640,128]{1,2,0:T(8,128)(2,1)S(1)} %copy.8), channel_id=1, source_target_pairs={{0,28},{4,0},{8,4},{12,8},{16,12},{20,16},{24,20},{28,24},{1,29},{... | collective-permute-start | bytes 1966088 | tf_op jit(solution)/shard_map/ppermute | solution.py:42
  39.0 29.7 %collective-permute-start.2 = (bf16[4,640,128]{1,2,0:T(8,128)(2,1)S(1)}, bf16[4,640,128]{1,2,0:T(8,128)(2,1)S(1)}, u32[]{:S(2)}, u32[]{:S(2)}) collective-permute-start(bf16[4,640,128]{1,2,0:T(8,128)(2,1)S(1)} %collective-permute-done), channel_id=1, source_target_pairs={{0,4},{4,8},{8,12},{12,16},{16,20},{20,24},{24,28},{28,0},{1,5},{5... | collective-permute-start | bytes 1966088 | tf_op jit(solution)/shard_map/ppermute | solution.py:37
  51.0 35.6 %collective-permute-start.3 = (bf16[4,640,128]{1,2,0:T(8,128)(2,1)S(1)}, bf16[4,640,128]{1,2,0:T(8,128)(2,1)}, u32[]{:S(2)}, u32[]{:S(2)}) collective-permute-start(bf16[4,640,128]{1,2,0:T(8,128)(2,1)S(1)} %collective-permute-done.1), channel_id=1, source_target_pairs={{0,28},{4,0},{8,4},{12,8},{16,12},{20,16},{24,20},{28,24},{1,29},{... | collective-permute-start | bytes 1966088 | tf_op jit(solution)/shard_map/ppermute | solution.py:42
  68.7 30.9 %collective-permute-start.4 = (bf16[4,640,128]{1,2,0:T(8,128)(2,1)S(1)}, bf16[4,640,128]{1,2,0:T(8,128)(2,1)S(1)}, u32[]{:S(2)}, u32[]{:S(2)}) collective-permute-start(bf16[4,640,128]{1,2,0:T(8,128)(2,1)S(1)} %collective-permute-done.2), channel_id=1, source_target_pairs={{0,4},{4,8},{8,12},{12,16},{16,20},{20,24},{24,28},{28,0},{1,5},{5... | collective-permute-start | bytes 1966088 | tf_op jit(solution)/shard_map/ppermute | solution.py:37
  86.6 31.0 %collective-permute-start.5 = (bf16[4,640,128]{1,2,0:T(8,128)(2,1)}, bf16[4,640,128]{1,2,0:T(8,128)(2,1)}, u32[]{:S(2)}, u32[]{:S(2)}) collective-permute-start(bf16[4,640,128]{1,2,0:T(8,128)(2,1)} %collective-permute-done.3), channel_id=1, source_target_pairs={{0,28},{4,0},{8,4},{12,8},{16,12},{20,16},{24,20},{28,24},{1,29},{... | collective-permute-start | bytes 1966088 | tf_op jit(solution)/shard_map/ppermute | solution.py:42
  99.6 20.1 %collective-permute-start.6 = (bf16[4,640,128]{1,2,0:T(8,128)(2,1)S(1)}, bf16[4,640,128]{1,2,0:T(8,128)(2,1)S(1)}, u32[]{:S(2)}, u32[]{:S(2)}) collective-permute-start(bf16[4,640,128]{1,2,0:T(8,128)(2,1)S(1)} %collective-permute-done.4), channel_id=1, source_target_pairs={{0,4},{4,8},{8,12},{12,16},{16,20},{20,24},{24,28},{28,0},{1,5},{5... | collective-permute-start | bytes 1966088 | tf_op jit(solution)/shard_map/ppermute | solution.py:37
  120.6 17.0 %slice-start = ((s8[20971520]{0:T(1024)(128)(4,1)}), s8[4194304]{0:T(1024)(128)(4,1)S(1)}, s32[]{:S(2)}) async-start(s8[20971520]{0:T(1024)(128)(4,1)} %bitcast.64), calls=%async_computation.6 | async-start | bytes 8388608
  120.6 17.0 %slice-start.1 = ((s8[20971520]{0:T(1024)(128)(4,1)}), s8[4194304]{0:T(1024)(128)(4,1)S(1)}, s32[]{:S(2)}) async-start(s8[20971520]{0:T(1024)(128)(4,1)} %bitcast.64), calls=%async_computation.7 | async-start | bytes 8388608
  128.6 9.0 %slice-start.2 = ((s8[20971520]{0:T(1024)(128)(4,1)}), s8[4194304]{0:T(1024)(128)(4,1)S(1)}, s32[]{:S(2)}) async-start(s8[20971520]{0:T(1024)(128)(4,1)} %bitcast.64), calls=%async_computation.8 | async-start | bytes 8388608
  130.6 7.0 %slice-start.3 = ((s8[20971520]{0:T(1024)(128)(4,1)}), s8[4194304]{0:T(1024)(128)(4,1)S(1)}, s32[]{:S(2)}) async-start(s8[20971520]{0:T(1024)(128)(4,1)} %bitcast.64), calls=%async_computation.9 | async-start | bytes 8388608
  130.6 7.0 %slice-start.4 = ((s8[20971520]{0:T(1024)(128)(4,1)}), s8[4194304]{0:T(1024)(128)(4,1)S(1)}, s32[]{:S(2)}) async-start(s8[20971520]{0:T(1024)(128)(4,1)} %bitcast.64), calls=%async_computation.10 | async-start | bytes 8388608
  142.4 4.1 copy-start.3
  146.6 4.7 %copy-start.6 = (f32[512,384]{0,1:T(8,128)S(1)}, f32[512,384]{0,1:T(8,128)}, u32[]{:S(2)}) copy-start(f32[512,384]{0,1:T(8,128)} %fusion.30) | copy-start | bytes 2359300
  146.6 4.7 %copy-start.7 = (f32[512,384]{0,1:T(8,128)S(1)}, f32[512,384]{0,1:T(8,128)}, u32[]{:S(2)}) copy-start(f32[512,384]{0,1:T(8,128)} %fusion.33) | copy-start | bytes 2359300
  151.2 1.1 copy-start.8
  152.7 7.6 %copy-start.9 = (f32[1,5120]{1,0:T(1,128)S(1)}, f32[1,5120]{1,0:T(1,128)}, u32[]{:S(2)}) copy-start(f32[1,5120]{1,0:T(1,128)} %get-tuple-element.24) | copy-start | bytes 61444
  166.3 112.5 %all-gather.3.cloned.1.call-start = ((), (), s32[]{:S(2)}) async-start(), calls=%async_computation.3 | async-start | bytes 1474560 | tf_op jit(solution)/shard_map/all_gather | solution.py:65
  236.5 135.6 %reduce-scatter.5.cloned.1.call-start = ((), (), s32[]{:S(2)}) async-start(), calls=%async_computation.4 | async-start | bytes 2949120 | tf_op jit(solution)/shard_map/reduce_scatter | solution.py:70
  290.4 10.0 %copy-start = (bf16[5120,128]{0,1:T(8,128)(2,1)S(1)}, bf16[5120,128]{0,1:T(8,128)(2,1)}, u32[]{:S(2)}) copy-start(bf16[5120,128]{0,1:T(8,128)(2,1)} %all-gather.3.cloned.1.call-done) | copy-start | bytes 3932164
  302.4 71.5 %copy-start.2 = (bf16[4,640,128]{2,1,0:T(8,128)(2,1)S(1)}, bf16[4,640,128]{2,1,0:T(8,128)(2,1)}, u32[]{:S(2)}) copy-start(bf16[4,640,128]{2,1,0:T(8,128)(2,1)} %param.3) | copy-start | bytes 1966084
  302.4 113.6 %all-gather.5.cloned.1.call-start = ((), (), s32[]{:S(2)}) async-start(), calls=%async_computation.5 | async-start | bytes 1474560 | tf_op jit(solution)/shard_map/all_gather | solution.py:76
  416.0 2.0 copy-start.1
  419.8 30.2 %copy-start.4 = (f32[640,128]{0,1:T(8,128)S(1)}, f32[640,128]{0,1:T(8,128)}, u32[]{:S(2)}) copy-start(f32[640,128]{0,1:T(8,128)} %reduce-scatter.3.cloned.1.call-done) | copy-start | bytes 983044
  419.8 30.1 %copy-start.5 = (f32[640,128]{0,1:T(8,128)S(1)}, f32[640,128]{0,1:T(8,128)}, u32[]{:S(2)}) copy-start(f32[640,128]{0,1:T(8,128)} %reduce-scatter.5.cloned.1.call-done) | copy-start | bytes 983044
Sparse Core Ops, SparseCore 0:
  166.5 68.3 reduce-scatter.2
  237.1 41.6 all-gather.2
  302.5 69.5 reduce-scatter.4
  374.3 41.6 all-gather.4
